TPU v7x, 256 devices: a whole 4x4x8 slice. The times are simulated.
256 devices in a mesh: group: 16 (over z, core), shard: 16 (over y, x).
Axes of the slice: x: 4, y: 4, z: 8, core: 2. Of those that a mesh axis runs over, the one named last changes fastest.
Arguments:
- tokens: bfloat16 [512, 1280], P(('group', 'shard')), as said below
- kv_cache: bfloat16 [512, 128, 2560], P(('group', 'shard'))
- keep_list: int32 [512, 128], P(('group', 'shard')), may hold values from 0 to 1
- lengths: int32 [512], P(('group', 'shard')), may hold values from 64 to 128
- merge_index: int32 [512, 128], P(('group', 'shard')), may hold values from 0 to 15
- merge_table: bfloat16 [16], replicated, may hold values from 0.0099487305 to 0.099609375
- move_offset: int32 [16, 2], P('shard'), may hold values from 0 to 15, as said below
- pair_mask: int32 [16], P('shard'), may hold values from 1 to 15
- w_qkv: bfloat16 [1280, 3840], P(None, 'shard'), may hold values from -0.15625 to 0.15625
- w_out: bfloat16 [1280, 1280], P(None, 'shard'), may hold values from -0.15625 to 0.15625
- w_up: bfloat16 [1280, 5120], P(None, 'shard'), may hold values from -0.15625 to 0.15625
- w_gate: bfloat16 [1280, 5120], P(None, 'shard'), may hold values from -0.15625 to 0.15625
- w_down: bfloat16 [5120, 1280], P('shard'), may hold values from -0.078125 to 0.078125
- qk_scale: float32 [1280], replicated, may hold values from 0.5 to 2
- attn_rate: float32 [1280], replicated, may hold values from 0.05 to 0.5
- mlp_rate: float32 [1280], replicated, may hold values from 0.05 to 0.5
- up_scale: float32 [5120], P('shard'), may hold values from 0.5 to 2
- gate_scale: float32 [5120], P('shard'), may hold values from 0.5 to 2
Outputs:
- new_hidden: bfloat16 [512, 1280], P(('group', 'shard'))
- moved_cache: bfloat16 [512, 128, 2560], P(('group', 'shard'))
Inputs may be any that keep to these rules, and one draw needn't show every extreme that they name: `tokens`: slot 1 of group g and shard s holds the same token as that slot of group g XOR pair_mask[s] on shard s. `move_offset`: the 2 offsets of one shard index are distinct.
All inputs are finite; a program needn't handle non-finite values.
Results may differ from a plain program's by a relative error of at most 0.011.
Values may be sent and summed in bfloat16 or wider, within the bound.
A program may use at most 128 MiB of HBM per device.

v0:
```python
import jax
import jax.numpy as jnp
from jax import lax
from jax.sharding import PartitionSpec as P

DH = 64
BLOCK = 128
WTAB = 16
EPSILON = 1e-06
NEGATIVE = -1e30


def rms_normal(vector):
    return vector * lax.rsqrt(jnp.mean(vector * vector, axis=-1, keepdims=True) + EPSILON)


def head_normal(vector, scaling):
    return vector * lax.rsqrt(jnp.sum(vector * vector, axis=-1, keepdims=True) + EPSILON) * scaling


def rounded(vector):
    return lax.optimization_barrier(vector.astype(jnp.bfloat16)).astype(jnp.float32)


def spread_columns(row_block, weight):
    columns = jnp.dot(
        lax.all_gather(row_block, "shard", axis=0, tiled=True),
        weight,
        preferred_element_type=jnp.float32,
    ).astype(jnp.bfloat16)
    return lax.all_to_all(columns, "shard", split_axis=0, concat_axis=1, tiled=True)


def compact_local(kv_cache, keep_list, lengths, merge_index, merge_table):
    slot_count, context, doubled = kv_cache.shape
    block_count = context // BLOCK
    in_length = jnp.arange(context, dtype=jnp.int32)[None, :] < lengths[:, None]
    keeper = (keep_list == 1) & in_length
    dropper = (keep_list == 0) & in_length
    position = jnp.cumsum(keeper.astype(jnp.int32), axis=1) - 1
    kept_count = jnp.sum(keeper.astype(jnp.int32), axis=1)
    drop_count = jnp.sum(dropper.astype(jnp.int32), axis=1)
    table_hits = merge_index[:, :, None] == jnp.arange(WTAB, dtype=jnp.int32)[None, None, :]
    weights = jnp.sum(
        jnp.where(table_hits, merge_table.astype(jnp.float32)[None, None, :], 0.0), axis=2
    ) * dropper.astype(jnp.float32)
    target = jnp.arange(BLOCK, dtype=jnp.int32)
    placing = (position[:, None, :] == target[None, :, None]) & keeper[:, None, :]
    summing = jnp.where(
        target[None, :, None] == kept_count[:, None, None], weights[:, None, :], 0.0
    )
    mixing = (placing.astype(jnp.float32) + summing).astype(jnp.bfloat16)
    packed = jnp.einsum(
        "ndk,nkc->ndc", mixing, kv_cache, preferred_element_type=jnp.float32
    ).astype(jnp.bfloat16)
    live_count = (kept_count + (drop_count > 0).astype(jnp.int32)).reshape(slot_count, block_count)
    return (packed, live_count.astype(jnp.bfloat16))


def per_device(
    tokens,
    kv_cache,
    keep_list,
    lengths,
    merge_index,
    merge_table,
    move_offset,
    pair_mask,
    w_qkv,
    w_out,
    w_up,
    w_gate,
    w_down,
    qk_scale,
    attn_rate,
    mlp_rate,
    up_scale,
    gate_scale,
):
    slot_count, context, doubled = kv_cache.shape
    model_width = tokens.shape[1]
    head_count = model_width // DH
    group_count = lax.axis_size("group")
    group_index = lax.axis_index("group")
    packed, live_count = compact_local(kv_cache, keep_list, lengths, merge_index, merge_table)
    offsets = move_offset[0]
    target = (group_index + offsets) % group_count
    sender = (jnp.arange(group_count, dtype=jnp.int32)[:, None] == target[None, :]).astype(
        jnp.bfloat16
    )
    outgoing = jnp.einsum("pj,jrc->prc", sender, packed, preferred_element_type=jnp.float32).astype(
        jnp.bfloat16
    )
    outgoing_live = jnp.einsum(
        "pj,jb->pb", sender, live_count, preferred_element_type=jnp.float32
    ).astype(jnp.bfloat16)
    incoming, incoming_live = (
        lax.all_to_all(outgoing, "group", split_axis=0, concat_axis=0, tiled=True),
        lax.all_to_all(outgoing_live, "group", split_axis=0, concat_axis=0, tiled=True),
    )
    source = (group_index - offsets) % group_count
    picker = (source[:, None] == jnp.arange(group_count, dtype=jnp.int32)[None, :]).astype(
        jnp.bfloat16
    )
    moved_cache = jnp.einsum(
        "jp,prc->jrc", picker, incoming, preferred_element_type=jnp.float32
    ).astype(jnp.bfloat16)
    moved_live = jnp.einsum("jp,pb->jb", picker, incoming_live, preferred_element_type=jnp.float32)
    projected = spread_columns(tokens, w_qkv)
    head_scale = qk_scale.reshape(head_count, DH)
    queries = head_normal(
        projected[:, :model_width].astype(jnp.float32).reshape(slot_count, head_count, DH),
        head_scale,
    ).astype(jnp.bfloat16)
    new_keys = head_normal(
        projected[:, model_width : 2 * model_width]
        .astype(jnp.float32)
        .reshape(slot_count, head_count, DH),
        head_scale,
    ).astype(jnp.bfloat16)
    new_values = projected[:, 2 * model_width :].reshape(slot_count, head_count, DH)
    key_rows = moved_cache[:, :, :model_width].reshape(slot_count, context, head_count, DH)
    value_rows = moved_cache[:, :, model_width:].reshape(slot_count, context, head_count, DH)
    score_scale = float(DH) ** 0.5
    scores = score_scale * jnp.einsum(
        "jhd,jrhd->jhr", queries, key_rows, preferred_element_type=jnp.float32
    )
    fresh_score = score_scale * jnp.sum(
        queries.astype(jnp.float32) * new_keys.astype(jnp.float32), axis=-1
    )
    row_valid = (jnp.arange(context, dtype=jnp.int32) % BLOCK).astype(jnp.float32)[
        None, :
    ] < jnp.repeat(moved_live, BLOCK, axis=1)
    pair_bits = pair_mask[0]
    partner = jnp.bitwise_xor(group_index, pair_bits)
    with_new = (jnp.arange(slot_count, dtype=jnp.int32) < slot_count - 1) | (group_index < partner)
    highest = jnp.maximum(
        jnp.max(jnp.where(row_valid[:, None, :], scores, NEGATIVE), axis=2),
        jnp.where(with_new[:, None], fresh_score, NEGATIVE),
    )
    safe_scores = jnp.where(row_valid[:, None, :], scores, highest[:, :, None])
    soft_weights = jnp.where(row_valid[:, None, :], jnp.exp(safe_scores - highest[:, :, None]), 0.0)
    fresh_weight = jnp.where(with_new[:, None], jnp.exp(fresh_score - highest), 0.0)
    weight_sum = jnp.sum(soft_weights, axis=2) + fresh_weight
    weighted = jnp.einsum(
        "jhr,jrhd->jhd",
        soft_weights.astype(jnp.bfloat16),
        value_rows,
        preferred_element_type=jnp.float32,
    )
    weighted = weighted + rounded(fresh_weight)[:, :, None] * new_values.astype(jnp.float32)
    last_high = highest[slot_count - 1 :]
    last_sum = weight_sum[slot_count - 1 :]
    last_weighted = weighted[slot_count - 1 :]
    gathered_high, gathered_sum, gathered_weighted = (
        lax.all_gather(last_high, "group", axis=0, tiled=True),
        lax.all_gather(last_sum, "group", axis=0, tiled=True),
        lax.all_gather(last_weighted, "group", axis=0, tiled=True),
    )
    picker_group = (jnp.arange(group_count, dtype=jnp.int32) == partner).astype(jnp.float32)
    other_high = jnp.sum(picker_group[:, None] * gathered_high, axis=0, keepdims=True)
    other_sum = jnp.sum(picker_group[:, None] * gathered_sum, axis=0, keepdims=True)
    other_weighted = jnp.sum(picker_group[:, None, None] * gathered_weighted, axis=0, keepdims=True)
    merged = jnp.maximum(last_high, other_high)
    own_factor = jnp.exp(last_high - merged)
    other_factor = jnp.exp(other_high - merged)
    long_sum = last_sum * own_factor + other_sum * other_factor
    long_weighted = (
        last_weighted * own_factor[:, :, None] + other_weighted * other_factor[:, :, None]
    )
    weight_sum = jnp.concatenate([weight_sum[: slot_count - 1], long_sum], axis=0)
    weighted = jnp.concatenate([weighted[: slot_count - 1], long_weighted], axis=0)
    attended = (
        (weighted / weight_sum[:, :, None]).reshape(slot_count, model_width).astype(jnp.bfloat16)
    )
    attention_out = spread_columns(attended, w_out)
    hidden = tokens.astype(jnp.float32)
    mixed = rms_normal(
        hidden + attn_rate * (rms_normal(attention_out.astype(jnp.float32)) - hidden)
    )
    mixed_low = mixed.astype(jnp.bfloat16)
    gate_factor = gate_scale * float(model_width) ** 0.5
    shard_rows = lax.all_gather(mixed_low, "shard", axis=0, tiled=True)
    up_part = jnp.dot(shard_rows, w_up, preferred_element_type=jnp.float32) * up_scale
    gate_part = jnp.dot(shard_rows, w_gate, preferred_element_type=jnp.float32) * gate_factor
    inner = (up_part * jax.nn.silu(gate_part)).astype(jnp.bfloat16)
    partial_terms = jnp.dot(inner, w_down, preferred_element_type=jnp.float32)
    mlp_out = lax.psum_scatter(
        partial_terms.astype(jnp.bfloat16), "shard", scatter_dimension=0, tiled=True
    ).astype(jnp.float32)
    new_hidden = rms_normal(mixed + mlp_rate * (rms_normal(mlp_out) - mixed)).astype(jnp.bfloat16)
    return (new_hidden, moved_cache)


def solution(mesh):
    return jax.shard_map(
        per_device,
        mesh=mesh,
        in_specs=(
            P(("group", "shard"), None),
            P(("group", "shard"), None, None),
            P(("group", "shard"), None),
            P(("group", "shard")),
            P(("group", "shard"), None),
            P(),
            P("shard", None),
            P("shard"),
            P(None, "shard"),
            P(None, "shard"),
            P(None, "shard"),
            P(None, "shard"),
            P("shard", None),
            P(),
            P(),
            P(),
            P("shard"),
            P("shard"),
        ),
        out_specs=(P(("group", "shard"), None), P(("group", "shard"), None, None)),
        check_vma=False,
    )
```

profile of v0, /device:TPU:32, one launch (start us, length us, event | category | flops | bytes accessed | tf_op | source)
XLA Modules:
  0.0 549.3 jit_solution(16223864282160331246)
XLA Ops:
  7.2 0.8 convert_element_type.140
  7.9 0.8 select_reduce_fusion.1
  8.7 0.8 fusion.64
  9.5 0.8 broadcast_select_fusion
  10.2 0.7 fusion.43
  10.9 0.1 convert_reduce_fusion
  11.1 0.2 fusion.9
  11.2 0.7 copy.91
  11.9 8.6 %all-to-all-start = ((bf16[16,1,1]{2,1,0:T(2,128)(2,1)}), bf16[16,1,1]{2,1,0:T(2,128)(2,1)S(1)}, u32[]{:S(2)}, u32[]{:S(2)}) async-start(bf16[16,1,1]{2,1,0:T(2,128)(2,1)} %copy.91), calls=%async_computation | async-start | bytes 16384 | tf_op jit(solution)/shard_map/all_to_all | solution.py:99
  20.6 0.3 reduce_window_sum.11
  20.9 23.9 %all-gather = bf16[16,2,1280]{2,1,0:T(2,128)(2,1)S(1)} all-gather(bf16[1,2,1280]{2,1,0:T(2,128)(2,1)} %bitcast.99), channel_id=1, replica_groups=mesh['group'=16,'shard'=16] {'shard'}, dimensions={0}, use_global_device_ids=true | all-gather | bytes 87040 | tf_op jit(solution)/shard_map/all_gather | solution.py:27
  44.9 1.3 convolution_convert_fusion.3
  46.2 0.6 convolution_convert_fusion.1
  46.8 0.6 all_to_all.35
  47.5 4.7 all-to-all-start.1
  52.1 6.1 %convolution_convert_fusion = bf16[16,128,2560]{2,0,1:T(8,128)(2,1)} fusion(bf16[2,128,2560]{2,1,0:T(8,128)(2,1)S(1)} %convolution_convert_fusion.1, s32[2]{0:T(128)S(1)} %fusion.43), kind=kOutput, calls=%fused_computation.2 | convolution fusion | flops 26214432 | bytes 11796488 | tf_op jit(solution)/shard_map/pj,jrc->prc/dot_general | solution.py:91
  58.2 13.7 %copy.94 = bf16[16,128,2560]{2,1,0:T(8,128)(2,1)} copy(bf16[16,128,2560]{2,0,1:T(8,128)(2,1)} %convolution_convert_fusion) | data formatting | bytes 20971520 | tf_op jit(solution)/shard_map/convert_element_type | solution.py:91
  72.0 7.4 %all-to-all-start.2 = ((bf16[16,128,2560]{2,1,0:T(8,128)(2,1)}), bf16[16,128,2560]{2,1,0:T(8,128)(2,1)}, u32[]{:S(2)}, u32[]{:S(2)}) async-start(bf16[16,128,2560]{2,1,0:T(8,128)(2,1)} %copy.94), calls=%async_computation.2 | async-start | bytes 20971520 | tf_op jit(solution)/shard_map/all_to_all | solution.py:98
  80.1 0.2 reduce.2
  80.3 0.2 convolution_bitcast_fusion
  80.6 0.1 all_to_all.38
  80.8 0.1 reshape.274
  80.8 0.1 reshape.272
  80.9 0.1 reshape.275
  81.0 0.1 multiply_reduce_fusion.2
  81.1 0.1 multiply_reduce_fusion.3
  81.2 0.2 multiply_reduce_fusion.1
  81.4 225.6 %all-to-all-done.2 = bf16[16,128,2560]{2,1,0:T(8,128)(2,1)} async-done(((bf16[16,128,2560]{2,1,0:T(8,128)(2,1)}), bf16[16,128,2560]{2,1,0:T(8,128)(2,1)}, u32[]{:S(2)}, u32[]{:S(2)}) %all-to-all-start.2) | async-done | bytes 10485792 | tf_op jit(solution)/shard_map/all_to_all | solution.py:98
  306.9 15.7 %fusion.2 = bf16[2,128,2560]{2,0,1:T(2,128)(2,1)S(1)} fusion(bf16[16,128,2560]{2,1,0:T(8,128)(2,1)} %all-to-all-done.2, s32[2]{0:T(128)S(1)} %and_select_fusion.1), kind=kOutput, calls=%fused_computation.3 | convolution fusion | flops 21626912 | bytes 11796488 | tf_op jit(solution)/shard_map/jp,prc->jrc/dot_general | solution.py:105
  322.7 1.7 fusion.65
  324.4 3.0 copy.96
  327.3 1.4 fusion.25
  328.7 0.1 select_reduce_fusion
  328.8 0.1 copy.97
  329.0 0.1 copy.98
  329.1 15.7 %all-gather.1 = f32[16,1,20]{2,1,0:T(1,128)S(1)} all-gather(f32[1,1,20]{2,1,0:T(1,128)S(1)} %slice_bitcast_fusion.1), channel_id=1, replica_groups=mesh['group'=16,'shard'=16] {'group'}, dimensions={0}, use_global_device_ids=true | all-gather | bytes 1360 | tf_op jit(solution)/shard_map/all_gather | solution.py:156
  344.8 0.1 convert_bitcast_fusion.1
  344.9 0.1 reduce_sum.137
  345.0 0.1 copy.100
  345.1 15.6 %all-gather.2 = f32[16,1,20]{2,1,0:T(1,128)S(1)} all-gather(f32[1,1,20]{2,1,0:T(1,128)S(1)} %slice_bitcast_fusion), channel_id=1, replica_groups=mesh['group'=16,'shard'=16] {'group'}, dimensions={0}, use_global_device_ids=true | all-gather | bytes 1360 | tf_op jit(solution)/shard_map/all_gather | solution.py:157
  360.7 0.1 multiply_reduce_fusion.7
  360.9 0.1 div.28
  361.0 1.9 copy.99
  362.9 1.5 fusion.23
  364.5 15.2 %all_gather.20 = f32[16,20,64]{2,1,0:T(8,128)S(1)} all-gather(f32[1,20,64]{2,1,0:T(8,128)S(1)} %slice.46), channel_id=1, replica_groups=mesh['group'=16,'shard'=16] {'group'}, dimensions={0}, use_global_device_ids=true | all-gather | bytes 87040 | tf_op jit(solution)/shard_map/all_gather | solution.py:158
  379.7 0.1 multiply_reduce_fusion
  380.1 25.8 %all-gather.3 = bf16[16,2,1280]{2,1,0:T(2,128)(2,1)} all-gather(bf16[1,2,1280]{2,1,0:T(2,128)(2,1)S(1)} %fusion.36), channel_id=1, replica_groups=mesh['group'=16,'shard'=16] {'shard'}, dimensions={0}, use_global_device_ids=true | all-gather | bytes 87040 | tf_op jit(solution)/shard_map/all_gather | solution.py:27
  405.9 0.9 reshape.284
  406.8 1.7 convolution_convert_fusion.4
  408.6 4.6 all-to-all-start.3
  413.2 7.4 %all-to-all-done.3 = bf16[16,2,80]{2,1,0:T(2,128)(2,1)S(1)} async-done(((bf16[16,2,80]{2,1,0:T(2,128)(2,1)}), bf16[16,2,80]{2,1,0:T(2,128)(2,1)S(1)}, u32[]{:S(2)}, u32[]{:S(2)}) %all-to-all-start.3) | async-done | bytes 5152 | tf_op jit(solution)/shard_map/all_to_all | solution.py:31
  420.6 0.1 reshape.276
  420.7 0.1 fusion.27
  420.9 0.2 multiply_reduce_fusion.5
  421.2 23.5 %all-gather.4 = bf16[16,2,1280]{2,1,0:T(2,128)(2,1)} all-gather(bf16[1,2,1280]{2,1,0:T(2,128)(2,1)S(1)} %fusion.35), channel_id=1, replica_groups=mesh['group'=16,'shard'=16] {'shard'}, dimensions={0}, use_global_device_ids=true | all-gather | bytes 87040 | tf_op jit(solution)/shard_map/all_gather | solution.py:183
  444.6 0.9 reshape.286
  445.6 2.1 convolution_multiply_fusion
  447.7 2.6 convolution_convert_fusion.2
  450.3 0.6 dynamic-slice
  451.5 1.2 copy.102
  452.7 87.3 %all-reduce.3.cloned.1.call-done = bf16[32,1280]{1,0:T(8,128)(2,1)} async-done(((bf16[32,1280]{1,0:T(8,128)(2,1)}), bf16[32,1280]{1,0:T(8,128)(2,1)}) %all-reduce.3.cloned.1.call-update) | async-done | bytes 81936
  540.0 0.9 fusion.30
  540.9 0.9 multiply_reduce_fusion.4
  541.8 0.7 multiply_convert_fusion.2
  (56 shorter events, 1.1 us)
Async XLA Ops:
  7.2 39.1 %copy-start = (bf16[2,128,2560]{2,1,0:T(8,128)(2,1)S(1)}, bf16[2,128,2560]{2,1,0:T(8,128)(2,1)}, u32[]{:S(2)}) copy-start(bf16[2,128,2560]{2,1,0:T(8,128)(2,1)} %param.19) | copy-start | bytes 3932164
  11.9 35.5 %all-to-all-start = ((bf16[16,1,1]{2,1,0:T(2,128)(2,1)}), bf16[16,1,1]{2,1,0:T(2,128)(2,1)S(1)}, u32[]{:S(2)}, u32[]{:S(2)}) async-start(bf16[16,1,1]{2,1,0:T(2,128)(2,1)} %copy.91), calls=%async_computation | async-start | bytes 16384 | tf_op jit(solution)/shard_map/all_to_all | solution.py:99
  47.5 24.5 %all-to-all-start.1 = ((bf16[16,2,240]{2,1,0:T(2,128)(2,1)}), bf16[16,2,240]{2,1,0:T(2,128)(2,1)S(1)}, u32[]{:S(2)}, u32[]{:S(2)}) async-start(bf16[16,2,240]{2,1,0:T(2,128)(2,1)} %all_to_all.35), calls=%async_computation.1 | async-start | bytes 32768 | tf_op jit(solution)/shard_map/all_to_all | solution.py:31
  72.0 7.4 %copy-start.4 = (f32[1280]{0:T(1024)S(1)}, f32[1280]{0:T(1024)}, u32[]{:S(2)}) copy-start(f32[1280]{0:T(1024)} %param.31) | copy-start | bytes 15364
  72.0 8.1 %copy-start.7 = (s32[1,2]{1,0:T(1,128)S(1)}, s32[1,2]{1,0:T(1,128)}, u32[]{:S(2)}) copy-start(s32[1,2]{1,0:T(1,128)} %param.24) | copy-start | bytes 28
  72.0 235.0 %all-to-all-start.2 = ((bf16[16,128,2560]{2,1,0:T(8,128)(2,1)}), bf16[16,128,2560]{2,1,0:T(8,128)(2,1)}, u32[]{:S(2)}, u32[]{:S(2)}) async-start(bf16[16,128,2560]{2,1,0:T(8,128)(2,1)} %copy.94), calls=%async_computation.2 | async-start | bytes 20971520 | tf_op jit(solution)/shard_map/all_to_all | solution.py:98
  361.0 52.2 %copy-start.6 = (f32[320]{0:T(512)S(1)}, f32[320]{0:T(512)}, u32[]{:S(2)}) copy-start(f32[320]{0:T(512)} %param.35) | copy-start | bytes 3844
  362.9 58.0 %copy-start.2 = (bf16[2,1280]{1,0:T(2,128)(2,1)S(1)}, bf16[2,1280]{1,0:T(2,128)(2,1)}, u32[]{:S(2)}) copy-start(bf16[2,1280]{1,0:T(2,128)(2,1)} %param.18) | copy-start | bytes 15364
  362.9 58.0 %copy-start.3 = (f32[1280]{0:T(1024)S(1)}, f32[1280]{0:T(1024)}, u32[]{:S(2)}) copy-start(f32[1280]{0:T(1024)} %param.32) | copy-start | bytes 15364
  364.4 83.3 %copy-start.1 = (bf16[320,1280]{1,0:T(8,128)(2,1)S(1)}, bf16[320,1280]{1,0:T(8,128)(2,1)}, u32[]{:S(2)}) copy-start(bf16[320,1280]{1,0:T(8,128)(2,1)} %param.30) | copy-start | bytes 2457604
  408.6 12.0 %all-to-all-start.3 = ((bf16[16,2,80]{2,1,0:T(2,128)(2,1)}), bf16[16,2,80]{2,1,0:T(2,128)(2,1)S(1)}, u32[]{:S(2)}, u32[]{:S(2)}) async-start(bf16[16,2,80]{2,1,0:T(2,128)(2,1)} %bitcast.27), calls=%async_computation.3 | async-start | bytes 16384 | tf_op jit(solution)/shard_map/all_to_all | solution.py:31
  413.1 126.9 %all-reduce.3.cloned.1.call-start = ((), (), s32[]{:S(2)}) async-start(), calls=%async_computation.4 | async-start | bytes 163840
  445.6 4.7 copy-start.8
  451.5 89.3 %copy-start.5 = (f32[1280]{0:T(1024)S(1)}, f32[1280]{0:T(1024)}, u32[]{:S(2)}) copy-start(f32[1280]{0:T(1024)} %param.33) | copy-start | bytes 15364
Sparse Core Ops, SparseCore 0:
  450.4 89.5 all-reduce.2
where the time goes:
time: 550 us; the launch traced here: 549 us
  waiting for transfers between devices  320 us (58%)
  blocking collectives  120 us (22%)
  matrix products  33.4 us (6%)
  local copies, waits for them, and re-layouts  26.5 us (5%)
  starting transfers between devices  25.2 us (5%)
  between operations  15.6 us (3%)
  other arithmetic  8.59 us (2%)
    all_to_all x1, waiting for transfers between devices, per_device(): lax.all_to_all(outgoing, 'group', split_axis=0, concat_axis=0, tiled=True)  226 us
    unnamed x2, waiting for transfers between devices  87.3 us
    all_gather x2, blocking collectives, spread_columns(): lax.all_gather(row_block, 'shard', axis=0, tiled=True)  49.7 us
    all_gather x1, blocking collectives, per_device(): shard_rows = lax.all_gather(mixed_low, 'shard', axis=0, tiled=True)  23.5 us
    all_gather x1, blocking collectives, per_device(): lax.all_gather(last_high, 'group', axis=0, tiled=True)  15.7 us
    dot_general x1, matrix products, per_device(): jnp.einsum('jp,prc->jrc', picker, incoming, preferred_element_type=jnp.fl...  15.7 us
    all_gather x1, blocking collectives, per_device(): lax.all_gather(last_sum, 'group', axis=0, tiled=True)  15.6 us
    all_gather x1, blocking collectives, per_device(): lax.all_gather(last_weighted, 'group', axis=0, tiled=True)  15.2 us
  transfers between devices with their start and end apart: 5, of which 3 were waited for; matrix products, arithmetic and copies ran while one was open for 5% of the time, Pallas kernels for 0%

commit v1 on v0

--- a/solution.py
+++ b/solution.py
@@ -180,7 +180,14 @@
     )
     mixed_low = mixed.astype(jnp.bfloat16)
     gate_factor = gate_scale * float(model_width) ** 0.5
-    shard_rows = lax.all_gather(mixed_low, "shard", axis=0, tiled=True)
+    ring = [mixed_low]
+    for hop in range(15):
+        ring.append(lax.ppermute(ring[-1], "shard", [(dev, (dev + 1) % 16) for dev in range(16)]))
+    shard_rows = jnp.roll(
+        jnp.concatenate(ring[::-1], axis=0),
+        (lax.axis_index("shard") + 1) * ring[0].shape[0],
+        axis=0,
+    )
     up_part = jnp.dot(shard_rows, w_up, preferred_element_type=jnp.float32) * up_scale
     gate_part = jnp.dot(shard_rows, w_gate, preferred_element_type=jnp.float32) * gate_factor
     inner = (up_part * jax.nn.silu(gate_part)).astype(jnp.bfloat16)

time: 550 us -> 642 us (1.17); the launches traced: 549 us -> 634 us
  waiting for transfers between devices: 320 us -> 413 us
  blocking collectives: 120 us -> 108 us
  local copies, waits for them, and re-layouts: 26.5 us -> 33.9 us
    ppermute x0 -> x15, waiting for transfers between devices: none -> 103 us  [per_device(): lax.ppermute(ring[-1], 'shard', [(dev, (dev + 1) % 16) for dev in range(1...]
    all_gather x1 -> x0, blocking collectives: 23.5 us -> none  [per_device(): shard_rows = lax.all_gather(mixed_low, 'shard', axis=0, tiled=True)]
    all_to_all x0 -> x1, blocking collectives: none -> 12 us  [spread_columns(): lax.all_to_all(columns, 'shard', split_axis=0, concat_axis=1, tiled=True)]
    all_to_all x2 -> x1, waiting for transfers between devices: 7.41 us -> 0.01 us  [spread_columns(): lax.all_to_all(columns, 'shard', split_axis=0, concat_axis=1, tiled=True)]
    concatenate x0 -> x1, local copies, waits for them, and re-layouts: none -> 6.66 us  [per_device(): jnp.roll(jnp.concatenate(ring[::-1], axis=0), (lax.axis_index('shard') +...]
  transfers between devices with their start and end apart: 5 -> 19, of which waited for: 3 -> 17; matrix products, arithmetic and copies ran while one was open for 5% -> 4% of each run, Pallas kernels for 0% -> 0%
where the time goes in v1:
time: 642 us; the launch traced here: 634 us
  waiting for transfers between devices  413 us (64%)
  blocking collectives  108 us (17%)
  local copies, waits for them, and re-layouts  33.9 us (5%)
  matrix products  32.1 us (5%)
  starting transfers between devices  22 us (3%)
  between operations  15.8 us (2%)
  other arithmetic  9.27 us (1%)
    all_to_all x1, waiting for transfers between devices, per_device(): lax.all_to_all(outgoing, 'group', split_axis=0, concat_axis=0, tiled=True)  225 us
    ppermute x15, waiting for transfers between devices, per_device(): lax.ppermute(ring[-1], 'shard', [(dev, (dev + 1) % 16) for dev in range(1...  103 us
    unnamed x2, waiting for transfers between devices  84.9 us
    all_gather x2, blocking collectives, spread_columns(): lax.all_gather(row_block, 'shard', axis=0, tiled=True)  49.7 us
    all_gather x1, blocking collectives, per_device(): lax.all_gather(last_high, 'group', axis=0, tiled=True)  15.7 us
    dot_general x1, matrix products, per_device(): jnp.einsum('jp,prc->jrc', picker, incoming, preferred_element_type=jnp.fl...  15.7 us
    all_gather x1, blocking collectives, per_device(): lax.all_gather(last_sum, 'group', axis=0, tiled=True)  15.6 us
    all_gather x1, blocking collectives, per_device(): lax.all_gather(last_weighted, 'group', axis=0, tiled=True)  15.1 us
  transfers between devices with their start and end apart: 19, of which 17 were waited for; matrix products, arithmetic and copies ran while one was open for 4% of the time, Pallas kernels for 0%

profile of v1, /device:TPU:32, one launch (start us, length us, event | category | flops | bytes accessed | tf_op | source)
XLA Modules:
  0.0 634.4 jit_solution(11099043477280781301)
XLA Ops:
  7.2 0.8 convert_element_type.140
  7.9 0.8 select_reduce_fusion.1
  8.7 0.8 fusion.69
  9.5 0.8 broadcast_select_fusion
  10.2 0.7 fusion.45
  11.2 0.7 copy.91
  11.9 8.6 %all-to-all-start = ((bf16[16,1,1]{2,1,0:T(2,128)(2,1)}), bf16[16,1,1]{2,1,0:T(2,128)(2,1)S(1)}, u32[]{:S(2)}, u32[]{:S(2)}) async-start(bf16[16,1,1]{2,1,0:T(2,128)(2,1)} %copy.91), calls=%async_computation | async-start | bytes 16384 | tf_op jit(solution)/shard_map/all_to_all | solution.py:99
  20.6 0.3 reduce_window_sum.11
  20.9 23.9 %all-gather = bf16[16,2,1280]{2,1,0:T(2,128)(2,1)S(1)} all-gather(bf16[1,2,1280]{2,1,0:T(2,128)(2,1)} %bitcast.96), channel_id=1, replica_groups=mesh['group'=16,'shard'=16] {'shard'}, dimensions={0}, use_global_device_ids=true | all-gather | bytes 87040 | tf_op jit(solution)/shard_map/all_gather | solution.py:27
  44.9 1.3 convolution_convert_fusion.3
  46.2 0.6 convolution_convert_fusion.1
  46.8 0.6 all_to_all.35
  47.5 4.7 all-to-all-start.1
  52.2 6.1 convolution_convert_fusion
  58.2 13.7 %copy.94 = bf16[16,128,2560]{2,1,0:T(8,128)(2,1)} copy(bf16[16,128,2560]{2,0,1:T(8,128)(2,1)} %convolution_convert_fusion) | data formatting | bytes 20971520 | tf_op jit(solution)/shard_map/convert_element_type | solution.py:91
  72.0 7.4 %all-to-all-start.2 = ((bf16[16,128,2560]{2,1,0:T(8,128)(2,1)}), bf16[16,128,2560]{2,1,0:T(8,128)(2,1)}, u32[]{:S(2)}, u32[]{:S(2)}) async-start(bf16[16,128,2560]{2,1,0:T(8,128)(2,1)} %copy.94), calls=%async_computation.2 | async-start | bytes 20971520 | tf_op jit(solution)/shard_map/all_to_all | solution.py:98
  79.3 0.5 all-reduce.3.cloned.1.call-start
  80.7 0.2 reduce.2
  80.9 0.2 convolution_bitcast_fusion
  81.9 225.1 %all-to-all-done.2 = bf16[16,128,2560]{2,1,0:T(8,128)(2,1)} async-done(((bf16[16,128,2560]{2,1,0:T(8,128)(2,1)}), bf16[16,128,2560]{2,1,0:T(8,128)(2,1)}, u32[]{:S(2)}, u32[]{:S(2)}) %all-to-all-start.2) | async-done | bytes 10485792 | tf_op jit(solution)/shard_map/all_to_all | solution.py:98
  306.9 15.7 %fusion.2 = bf16[2,128,2560]{2,0,1:T(2,128)(2,1)S(1)} fusion(bf16[16,128,2560]{2,1,0:T(8,128)(2,1)} %all-to-all-done.2, s32[2]{0:T(128)S(1)} %and_select_fusion.1), kind=kOutput, calls=%fused_computation.3 | convolution fusion | flops 21626912 | bytes 11796488 | tf_op jit(solution)/shard_map/jp,prc->jrc/dot_general | solution.py:105
  322.6 1.7 fusion.70
  324.3 3.0 copy.96
  327.3 1.4 fusion.28
  329.0 15.7 %all-gather.1 = f32[16,1,20]{2,1,0:T(1,128)S(1)} all-gather(f32[1,1,20]{2,1,0:T(1,128)S(1)} %slice_bitcast_fusion.1), channel_id=1, replica_groups=mesh['group'=16,'shard'=16] {'group'}, dimensions={0}, use_global_device_ids=true | all-gather | bytes 1360 | tf_op jit(solution)/shard_map/all_gather | solution.py:156
  345.1 15.6 %all-gather.2 = f32[16,1,20]{2,1,0:T(1,128)S(1)} all-gather(f32[1,1,20]{2,1,0:T(1,128)S(1)} %slice_bitcast_fusion), channel_id=1, replica_groups=mesh['group'=16,'shard'=16] {'group'}, dimensions={0}, use_global_device_ids=true | all-gather | bytes 1360 | tf_op jit(solution)/shard_map/all_gather | solution.py:157
  360.9 1.9 copy.99
  362.8 1.6 fusion.26
  364.5 15.1 %all_gather.17 = f32[16,20,64]{2,1,0:T(8,128)S(1)} all-gather(f32[1,20,64]{2,1,0:T(8,128)S(1)} %slice.46), channel_id=1, replica_groups=mesh['group'=16,'shard'=16] {'group'}, dimensions={0}, use_global_device_ids=true | all-gather | bytes 87040 | tf_op jit(solution)/shard_map/all_gather | solution.py:158
  380.0 25.8 %all-gather.3 = bf16[16,2,1280]{2,1,0:T(2,128)(2,1)} all-gather(bf16[1,2,1280]{2,1,0:T(2,128)(2,1)S(1)} %fusion.38), channel_id=1, replica_groups=mesh['group'=16,'shard'=16] {'shard'}, dimensions={0}, use_global_device_ids=true | all-gather | bytes 87040 | tf_op jit(solution)/shard_map/all_gather | solution.py:27
  405.7 0.9 reshape.284
  406.6 1.1 convolution_convert_fusion.4
  407.7 12.0 %all_to_all.46 = bf16[16,2,80]{2,1,0:T(2,128)(2,1)S(1)} all-to-all(bf16[16,2,80]{2,1,0:T(2,128)(2,1)S(1)} %bitcast.93), channel_id=1, replica_groups=mesh['group'=16,'shard'=16] {'shard'}, dimensions={0} | all-to-all | bytes 10240 | tf_op jit(solution)/shard_map/all_to_all | solution.py:31
  420.0 0.2 multiply_reduce_fusion.5
  420.2 0.6 copy-done.8
  420.8 0.6 collective-permute-start
  421.4 6.4 %collective-permute-done = bf16[2,1280]{1,0:T(2,128)(2,1)S(1)} collective-permute-done((bf16[2,1280]{1,0:T(2,128)(2,1)S(1)}, bf16[2,1280]{1,0:T(2,128)(2,1)S(1)}, u32[]{:S(2)}, u32[]{:S(2)}) %collective-permute-start) | collective-permute-done | bytes 5152 | tf_op jit(solution)/shard_map/ppermute | solution.py:185
  427.8 6.9 %collective-permute-done.1 = bf16[2,1280]{1,0:T(2,128)(2,1)S(1)} collective-permute-done((bf16[2,1280]{1,0:T(2,128)(2,1)S(1)}, bf16[2,1280]{1,0:T(2,128)(2,1)S(1)}, u32[]{:S(2)}, u32[]{:S(2)}) %collective-permute-start.1) | collective-permute-done | bytes 5152 | tf_op jit(solution)/shard_map/ppermute | solution.py:185
  434.7 6.9 %collective-permute-done.2 = bf16[2,1280]{1,0:T(2,128)(2,1)S(1)} collective-permute-done((bf16[2,1280]{1,0:T(2,128)(2,1)S(1)}, bf16[2,1280]{1,0:T(2,128)(2,1)S(1)}, u32[]{:S(2)}, u32[]{:S(2)}) %collective-permute-start.2) | collective-permute-done | bytes 5152 | tf_op jit(solution)/shard_map/ppermute | solution.py:185
  441.7 6.9 %collective-permute-done.3 = bf16[2,1280]{1,0:T(2,128)(2,1)S(1)} collective-permute-done((bf16[2,1280]{1,0:T(2,128)(2,1)S(1)}, bf16[2,1280]{1,0:T(2,128)(2,1)S(1)}, u32[]{:S(2)}, u32[]{:S(2)}) %collective-permute-start.3) | collective-permute-done | bytes 5152 | tf_op jit(solution)/shard_map/ppermute | solution.py:185
  448.6 6.9 %collective-permute-done.4 = bf16[2,1280]{1,0:T(2,128)(2,1)S(1)} collective-permute-done((bf16[2,1280]{1,0:T(2,128)(2,1)S(1)}, bf16[2,1280]{1,0:T(2,128)(2,1)S(1)}, u32[]{:S(2)}, u32[]{:S(2)}) %collective-permute-start.4) | collective-permute-done | bytes 5152 | tf_op jit(solution)/shard_map/ppermute | solution.py:185
  455.5 6.9 %collective-permute-done.5 = bf16[2,1280]{1,0:T(2,128)(2,1)S(1)} collective-permute-done((bf16[2,1280]{1,0:T(2,128)(2,1)S(1)}, bf16[2,1280]{1,0:T(2,128)(2,1)S(1)}, u32[]{:S(2)}, u32[]{:S(2)}) %collective-permute-start.5) | collective-permute-done | bytes 5152 | tf_op jit(solution)/shard_map/ppermute | solution.py:185
  462.5 6.9 %collective-permute-done.6 = bf16[2,1280]{1,0:T(2,128)(2,1)S(1)} collective-permute-done((bf16[2,1280]{1,0:T(2,128)(2,1)S(1)}, bf16[2,1280]{1,0:T(2,128)(2,1)S(1)}, u32[]{:S(2)}, u32[]{:S(2)}) %collective-permute-start.6) | collective-permute-done | bytes 5152 | tf_op jit(solution)/shard_map/ppermute | solution.py:185
  469.4 6.9 %collective-permute-done.7 = bf16[2,1280]{1,0:T(2,128)(2,1)S(1)} collective-permute-done((bf16[2,1280]{1,0:T(2,128)(2,1)S(1)}, bf16[2,1280]{1,0:T(2,128)(2,1)S(1)}, u32[]{:S(2)}, u32[]{:S(2)}) %collective-permute-start.7) | collective-permute-done | bytes 5152 | tf_op jit(solution)/shard_map/ppermute | solution.py:185
  476.4 6.9 %collective-permute-done.8 = bf16[2,1280]{1,0:T(2,128)(2,1)S(1)} collective-permute-done((bf16[2,1280]{1,0:T(2,128)(2,1)S(1)}, bf16[2,1280]{1,0:T(2,128)(2,1)S(1)}, u32[]{:S(2)}, u32[]{:S(2)}) %collective-permute-start.8) | collective-permute-done | bytes 5152 | tf_op jit(solution)/shard_map/ppermute | solution.py:185
  483.3 6.9 %collective-permute-done.9 = bf16[2,1280]{1,0:T(2,128)(2,1)S(1)} collective-permute-done((bf16[2,1280]{1,0:T(2,128)(2,1)S(1)}, bf16[2,1280]{1,0:T(2,128)(2,1)S(1)}, u32[]{:S(2)}, u32[]{:S(2)}) %collective-permute-start.9) | collective-permute-done | bytes 5152 | tf_op jit(solution)/shard_map/ppermute | solution.py:185
  490.2 0.2 collective-permute-start.10
  490.4 6.9 %collective-permute-done.10 = bf16[2,1280]{1,0:T(2,128)(2,1)S(1)} collective-permute-done((bf16[2,1280]{1,0:T(2,128)(2,1)S(1)}, bf16[2,1280]{1,0:T(2,128)(2,1)S(1)}, u32[]{:S(2)}, u32[]{:S(2)}) %collective-permute-start.10) | collective-permute-done | bytes 5152 | tf_op jit(solution)/shard_map/ppermute | solution.py:185
  497.4 6.9 %collective-permute-done.11 = bf16[2,1280]{1,0:T(2,128)(2,1)S(1)} collective-permute-done((bf16[2,1280]{1,0:T(2,128)(2,1)S(1)}, bf16[2,1280]{1,0:T(2,128)(2,1)S(1)}, u32[]{:S(2)}, u32[]{:S(2)}) %collective-permute-start.11) | collective-permute-done | bytes 5152 | tf_op jit(solution)/shard_map/ppermute | solution.py:185
  504.3 0.6 copy-done.3
  504.9 6.9 %collective-permute-done.12 = bf16[2,1280]{1,0:T(2,128)(2,1)S(1)} collective-permute-done((bf16[2,1280]{1,0:T(2,128)(2,1)S(1)}, bf16[2,1280]{1,0:T(2,128)(2,1)S(1)}, u32[]{:S(2)}, u32[]{:S(2)}) %collective-permute-start.12) | collective-permute-done | bytes 5152 | tf_op jit(solution)/shard_map/ppermute | solution.py:185
  511.8 0.6 copy-done.4
  512.4 7.0 %collective-permute-done.13 = bf16[2,1280]{1,0:T(2,128)(2,1)} collective-permute-done((bf16[2,1280]{1,0:T(2,128)(2,1)S(1)}, bf16[2,1280]{1,0:T(2,128)(2,1)}, u32[]{:S(2)}, u32[]{:S(2)}) %collective-permute-start.13) | collective-permute-done | bytes 5152 | tf_op jit(solution)/shard_map/ppermute | solution.py:185
  519.5 0.7 broadcast_multiply_fusion
  520.2 6.6 %collective-permute-done.14 = bf16[2,1280]{1,0:T(2,128)(2,1)} collective-permute-done((bf16[2,1280]{1,0:T(2,128)(2,1)}, bf16[2,1280]{1,0:T(2,128)(2,1)}, u32[]{:S(2)}, u32[]{:S(2)}) %collective-permute-start.14) | collective-permute-done | bytes 5152 | tf_op jit(solution)/shard_map/ppermute | solution.py:185
  526.7 6.7 %concatenate.21 = bf16[64,1280]{1,0:T(8,128)(2,1)} concatenate(bf16[2,1280]{1,0:T(2,128)(2,1)} %collective-permute-done.14, bf16[2,1280]{1,0:T(2,128)(2,1)} %collective-permute-done.13, bf16[2,1280]{1,0:T(2,128)(2,1)} %copy-done.4, bf16[2,1280]{1,0:T(2,128)(2,1)} %copy-done.3, bf16[2,1280]{1,0:T(2,128)(2,1)S(1)} %collective-permute-done.10, ...), dimensions={0} | concatenate | bytes 327680 | tf_op jit(solution)/shard_map/jit(_roll_dynamic)/concatenate | solution.py:186
  533.4 1.2 convolution_multiply_fusion
  534.7 2.8 convolution_convert_fusion.2
  537.5 0.6 dynamic-slice
  538.8 1.2 copy.102
  540.0 84.9 %all-reduce.3.cloned.1.call-done = bf16[32,1280]{1,0:T(8,128)(2,1)} async-done(((bf16[32,1280]{1,0:T(8,128)(2,1)}), bf16[32,1280]{1,0:T(8,128)(2,1)}) %all-reduce.3.cloned.1.call-update) | async-done | bytes 81936
  624.8 0.9 fusion.33
  625.7 0.9 multiply_reduce_fusion.4
  626.7 0.7 multiply_convert_fusion.2
  (90 shorter events, 3.1 us)
Async XLA Ops:
  7.2 39.1 %copy-start = (bf16[2,128,2560]{2,1,0:T(8,128)(2,1)S(1)}, bf16[2,128,2560]{2,1,0:T(8,128)(2,1)}, u32[]{:S(2)}) copy-start(bf16[2,128,2560]{2,1,0:T(8,128)(2,1)} %param.19) | copy-start | bytes 3932164
  11.9 35.5 %all-to-all-start = ((bf16[16,1,1]{2,1,0:T(2,128)(2,1)}), bf16[16,1,1]{2,1,0:T(2,128)(2,1)S(1)}, u32[]{:S(2)}, u32[]{:S(2)}) async-start(bf16[16,1,1]{2,1,0:T(2,128)(2,1)} %copy.91), calls=%async_computation | async-start | bytes 16384 | tf_op jit(solution)/shard_map/all_to_all | solution.py:99
  47.5 24.5 %all-to-all-start.1 = ((bf16[16,2,240]{2,1,0:T(2,128)(2,1)}), bf16[16,2,240]{2,1,0:T(2,128)(2,1)S(1)}, u32[]{:S(2)}, u32[]{:S(2)}) async-start(bf16[16,2,240]{2,1,0:T(2,128)(2,1)} %all_to_all.35), calls=%async_computation.1 | async-start | bytes 32768 | tf_op jit(solution)/shard_map/all_to_all | solution.py:31
  72.0 7.9 %copy-start.6 = (f32[1280]{0:T(1024)S(1)}, f32[1280]{0:T(1024)}, u32[]{:S(2)}) copy-start(f32[1280]{0:T(1024)} %param.31) | copy-start | bytes 15364
  72.0 8.7 %copy-start.10 = (s32[1,2]{1,0:T(1,128)S(1)}, s32[1,2]{1,0:T(1,128)}, u32[]{:S(2)}) copy-start(s32[1,2]{1,0:T(1,128)} %param.24) | copy-start | bytes 28
  72.0 235.0 %all-to-all-start.2 = ((bf16[16,128,2560]{2,1,0:T(8,128)(2,1)}), bf16[16,128,2560]{2,1,0:T(8,128)(2,1)}, u32[]{:S(2)}, u32[]{:S(2)}) async-start(bf16[16,128,2560]{2,1,0:T(8,128)(2,1)} %copy.94), calls=%async_computation.2 | async-start | bytes 20971520 | tf_op jit(solution)/shard_map/all_to_all | solution.py:98
  79.3 545.5 %all-reduce.3.cloned.1.call-start = ((), (), s32[]{:S(2)}) async-start(), calls=%async_computation.4 | async-start | bytes 163840
  362.8 57.2 %copy-start.2 = (bf16[2,1280]{1,0:T(2,128)(2,1)S(1)}, bf16[2,1280]{1,0:T(2,128)(2,1)}, u32[]{:S(2)}) copy-start(bf16[2,1280]{1,0:T(2,128)(2,1)} %param.18) | copy-start | bytes 15364
  362.8 57.2 %copy-start.5 = (f32[1280]{0:T(1024)S(1)}, f32[1280]{0:T(1024)}, u32[]{:S(2)}) copy-start(f32[1280]{0:T(1024)} %param.32) | copy-start | bytes 15364
  362.8 170.6 %copy-start.1 = (bf16[1280,320]{0,1:T(8,128)(2,1)S(1)}, bf16[1280,320]{0,1:T(8,128)(2,1)}, u32[]{:S(2)}) copy-start(bf16[1280,320]{0,1:T(8,128)(2,1)} %param.29) | copy-start | bytes 2457604
  420.2 0.6 copy-start.8
  420.8 7.0 %collective-permute-start = (bf16[2,1280]{1,0:T(2,128)(2,1)S(1)}, bf16[2,1280]{1,0:T(2,128)(2,1)S(1)}, u32[]{:S(2)}, u32[]{:S(2)}) collective-permute-start(bf16[2,1280]{1,0:T(2,128)(2,1)S(1)} %multiply_convert_fusion.3), channel_id=1, source_target_pairs={{0,1},{1,2},{2,3},{3,4},{4,5},{5,6},{6,7},{7,8},{8,9},{9,10},{10,1... | collective-permute-start | bytes 15368 | tf_op jit(solution)/shard_map/ppermute | solution.py:185
  427.8 6.9 %collective-permute-start.1 = (bf16[2,1280]{1,0:T(2,128)(2,1)S(1)}, bf16[2,1280]{1,0:T(2,128)(2,1)S(1)}, u32[]{:S(2)}, u32[]{:S(2)}) collective-permute-start(bf16[2,1280]{1,0:T(2,128)(2,1)S(1)} %collective-permute-done), channel_id=1, source_target_pairs={{0,1},{1,2},{2,3},{3,4},{4,5},{5,6},{6,7},{7,8},{8,9},{9,10},{10,1... | collective-permute-start | bytes 15368 | tf_op jit(solution)/shard_map/ppermute | solution.py:185
  434.7 6.9 %collective-permute-start.2 = (bf16[2,1280]{1,0:T(2,128)(2,1)S(1)}, bf16[2,1280]{1,0:T(2,128)(2,1)S(1)}, u32[]{:S(2)}, u32[]{:S(2)}) collective-permute-start(bf16[2,1280]{1,0:T(2,128)(2,1)S(1)} %collective-permute-done.1), channel_id=1, source_target_pairs={{0,1},{1,2},{2,3},{3,4},{4,5},{5,6},{6,7},{7,8},{8,9},{9,10},{10,1... | collective-permute-start | bytes 15368 | tf_op jit(solution)/shard_map/ppermute | solution.py:185
  441.7 6.9 %collective-permute-start.3 = (bf16[2,1280]{1,0:T(2,128)(2,1)S(1)}, bf16[2,1280]{1,0:T(2,128)(2,1)S(1)}, u32[]{:S(2)}, u32[]{:S(2)}) collective-permute-start(bf16[2,1280]{1,0:T(2,128)(2,1)S(1)} %collective-permute-done.2), channel_id=1, source_target_pairs={{0,1},{1,2},{2,3},{3,4},{4,5},{5,6},{6,7},{7,8},{8,9},{9,10},{10,1... | collective-permute-start | bytes 15368 | tf_op jit(solution)/shard_map/ppermute | solution.py:185
  448.6 6.9 %collective-permute-start.4 = (bf16[2,1280]{1,0:T(2,128)(2,1)S(1)}, bf16[2,1280]{1,0:T(2,128)(2,1)S(1)}, u32[]{:S(2)}, u32[]{:S(2)}) collective-permute-start(bf16[2,1280]{1,0:T(2,128)(2,1)S(1)} %collective-permute-done.3), channel_id=1, source_target_pairs={{0,1},{1,2},{2,3},{3,4},{4,5},{5,6},{6,7},{7,8},{8,9},{9,10},{10,1... | collective-permute-start | bytes 15368 | tf_op jit(solution)/shard_map/ppermute | solution.py:185
  455.5 6.9 %collective-permute-start.5 = (bf16[2,1280]{1,0:T(2,128)(2,1)S(1)}, bf16[2,1280]{1,0:T(2,128)(2,1)S(1)}, u32[]{:S(2)}, u32[]{:S(2)}) collective-permute-start(bf16[2,1280]{1,0:T(2,128)(2,1)S(1)} %collective-permute-done.4), channel_id=1, source_target_pairs={{0,1},{1,2},{2,3},{3,4},{4,5},{5,6},{6,7},{7,8},{8,9},{9,10},{10,1... | collective-permute-start | bytes 15368 | tf_op jit(solution)/shard_map/ppermute | solution.py:185
  462.5 6.9 %collective-permute-start.6 = (bf16[2,1280]{1,0:T(2,128)(2,1)S(1)}, bf16[2,1280]{1,0:T(2,128)(2,1)S(1)}, u32[]{:S(2)}, u32[]{:S(2)}) collective-permute-start(bf16[2,1280]{1,0:T(2,128)(2,1)S(1)} %collective-permute-done.5), channel_id=1, source_target_pairs={{0,1},{1,2},{2,3},{3,4},{4,5},{5,6},{6,7},{7,8},{8,9},{9,10},{10,1... | collective-permute-start | bytes 15368 | tf_op jit(solution)/shard_map/ppermute | solution.py:185
  469.4 6.9 %collective-permute-start.7 = (bf16[2,1280]{1,0:T(2,128)(2,1)S(1)}, bf16[2,1280]{1,0:T(2,128)(2,1)S(1)}, u32[]{:S(2)}, u32[]{:S(2)}) collective-permute-start(bf16[2,1280]{1,0:T(2,128)(2,1)S(1)} %collective-permute-done.6), channel_id=1, source_target_pairs={{0,1},{1,2},{2,3},{3,4},{4,5},{5,6},{6,7},{7,8},{8,9},{9,10},{10,1... | collective-permute-start | bytes 15368 | tf_op jit(solution)/shard_map/ppermute | solution.py:185
  476.4 6.9 %collective-permute-start.8 = (bf16[2,1280]{1,0:T(2,128)(2,1)S(1)}, bf16[2,1280]{1,0:T(2,128)(2,1)S(1)}, u32[]{:S(2)}, u32[]{:S(2)}) collective-permute-start(bf16[2,1280]{1,0:T(2,128)(2,1)S(1)} %collective-permute-done.7), channel_id=1, source_target_pairs={{0,1},{1,2},{2,3},{3,4},{4,5},{5,6},{6,7},{7,8},{8,9},{9,10},{10,1... | collective-permute-start | bytes 15368 | tf_op jit(solution)/shard_map/ppermute | solution.py:185
  483.3 6.9 %collective-permute-start.9 = (bf16[2,1280]{1,0:T(2,128)(2,1)S(1)}, bf16[2,1280]{1,0:T(2,128)(2,1)S(1)}, u32[]{:S(2)}, u32[]{:S(2)}) collective-permute-start(bf16[2,1280]{1,0:T(2,128)(2,1)S(1)} %collective-permute-done.8), channel_id=1, source_target_pairs={{0,1},{1,2},{2,3},{3,4},{4,5},{5,6},{6,7},{7,8},{8,9},{9,10},{10,1... | collective-permute-start | bytes 15368 | tf_op jit(solution)/shard_map/ppermute | solution.py:185
  490.2 7.1 %collective-permute-start.10 = (bf16[2,1280]{1,0:T(2,128)(2,1)S(1)}, bf16[2,1280]{1,0:T(2,128)(2,1)S(1)}, u32[]{:S(2)}, u32[]{:S(2)}) collective-permute-start(bf16[2,1280]{1,0:T(2,128)(2,1)S(1)} %collective-permute-done.9), channel_id=1, source_target_pairs={{0,1},{1,2},{2,3},{3,4},{4,5},{5,6},{6,7},{7,8},{8,9},{9,10},{10,1... | collective-permute-start | bytes 15368 | tf_op jit(solution)/shard_map/ppermute | solution.py:185
  497.4 6.9 %collective-permute-start.11 = (bf16[2,1280]{1,0:T(2,128)(2,1)S(1)}, bf16[2,1280]{1,0:T(2,128)(2,1)S(1)}, u32[]{:S(2)}, u32[]{:S(2)}) collective-permute-start(bf16[2,1280]{1,0:T(2,128)(2,1)S(1)} %collective-permute-done.10), channel_id=1, source_target_pairs={{0,1},{1,2},{2,3},{3,4},{4,5},{5,6},{6,7},{7,8},{8,9},{9,10},{10,1... | collective-permute-start | bytes 15368 | tf_op jit(solution)/shard_map/ppermute | solution.py:185
  504.3 0.6 copy-start.3
  504.9 6.9 %collective-permute-start.12 = (bf16[2,1280]{1,0:T(2,128)(2,1)S(1)}, bf16[2,1280]{1,0:T(2,128)(2,1)S(1)}, u32[]{:S(2)}, u32[]{:S(2)}) collective-permute-start(bf16[2,1280]{1,0:T(2,128)(2,1)S(1)} %collective-permute-done.11), channel_id=1, source_target_pairs={{0,1},{1,2},{2,3},{3,4},{4,5},{5,6},{6,7},{7,8},{8,9},{9,10},{10,1... | collective-permute-start | bytes 15368 | tf_op jit(solution)/shard_map/ppermute | solution.py:185
  511.8 0.6 copy-start.4
  512.4 7.0 %collective-permute-start.13 = (bf16[2,1280]{1,0:T(2,128)(2,1)S(1)}, bf16[2,1280]{1,0:T(2,128)(2,1)}, u32[]{:S(2)}, u32[]{:S(2)}) collective-permute-start(bf16[2,1280]{1,0:T(2,128)(2,1)S(1)} %collective-permute-done.12), channel_id=1, source_target_pairs={{0,1},{1,2},{2,3},{3,4},{4,5},{5,6},{6,7},{7,8},{8,9},{9,10},{10,1... | collective-permute-start | bytes 15368 | tf_op jit(solution)/shard_map/ppermute | solution.py:185
  519.5 7.3 %collective-permute-start.14 = (bf16[2,1280]{1,0:T(2,128)(2,1)}, bf16[2,1280]{1,0:T(2,128)(2,1)}, u32[]{:S(2)}, u32[]{:S(2)}) collective-permute-start(bf16[2,1280]{1,0:T(2,128)(2,1)} %collective-permute-done.13), channel_id=1, source_target_pairs={{0,1},{1,2},{2,3},{3,4},{4,5},{5,6},{6,7},{7,8},{8,9},{9,10},{10,1... | collective-permute-start | bytes 15368 | tf_op jit(solution)/shard_map/ppermute | solution.py:185
  533.4 4.1 copy-start.11
  538.8 86.9 %copy-start.7 = (f32[1280]{0:T(1024)S(1)}, f32[1280]{0:T(1024)}, u32[]{:S(2)}) copy-start(f32[1280]{0:T(1024)} %param.33) | copy-start | bytes 15364
  538.8 86.9 %copy-start.9 = (f32[2]{0:T(128)S(1)}, f32[2]{0:T(128)}, u32[]{:S(2)}) copy-start(f32[2]{0:T(128)} %copy-done.8) | copy-start | bytes 28
Sparse Core Ops, SparseCore 0:
  537.6 87.1 all-reduce.2
